TPU v7x, 32 devices: a whole 2x2x4 slice. The times are simulated.
32 devices in a mesh: dp: 8 (over z, x), mp: 4 (over y, core).
Axes of the slice: x: 2, y: 2, z: 4, core: 2. Of those that a mesh axis runs over, the one named last changes fastest.
Arguments:
- patches: bfloat16 [9216, 3072], P('dp'), may hold values from -6 to 6
- weight: bfloat16 [3072, 1536], P(None, 'mp'), may hold values from -0.109375 to 0.109375
- conv_bias: float32 [1536], P('mp'), may hold values from -3 to 3
- cotangent: bfloat16 [9216, 1536], P('dp', 'mp'), may hold values from -0.0390625 to 0.0390625
- row_scale: float32 [3072], replicated, may hold values from 0.25 to 4
- col_scale: float32 [1536], P('mp'), may hold values from 0.25 to 4
Outputs:
- output: bfloat16 [9216, 1536], P('dp', 'mp')
- left_factor: float32 [3072, 3072], P('dp', 'mp')
- right_factor: float32 [1536, 1536], P('dp', 'mp')
- norm_pair: float32 [2], replicated
All inputs are finite; a program needn't handle non-finite values.
Results may differ from a plain program's by a relative error of at most 0.001.
Values sent between devices are 32-bit elements; how exact they have to be, the bound alone decides.
A program may use at most 64 MiB of HBM per device.

v0:
```python
import jax
import jax.numpy as jnp
from jax import lax
from jax.sharding import PartitionSpec as P

COUT = 1536
K = 3072


def shards(patches, weight, conv_bias, cotangent, row_scale, col_scale):
    output = (jnp.dot(patches, weight, preferred_element_type=jnp.float32) + conv_bias).astype(
        jnp.bfloat16
    )
    inner_width = patches.shape[1]
    strip_rows = inner_width // lax.axis_size("dp")
    local_grad = lax.dot_general(
        patches, cotangent, (((0,), (0,)), ((), ())), preferred_element_type=jnp.float32
    )
    weighted = local_grad * row_scale[:, None] * col_scale[None, :]
    small_sum = jnp.sum(weighted * weighted)
    column = lax.psum(local_grad, "dp")
    rows_here = lax.dynamic_slice_in_dim(column, lax.axis_index("dp") * strip_rows, strip_rows, 0)
    left_part = lax.dot_general(
        rows_here,
        column,
        (((1,), (1,)), ((), ())),
        precision=lax.Precision.HIGHEST,
        preferred_element_type=jnp.float32,
    )
    left_factor = lax.psum_scatter(left_part / COUT, "mp", scatter_dimension=1, tiled=True)
    full_strip = lax.all_gather(rows_here, "mp", axis=1, tiled=True)
    right_factor = lax.psum_scatter(
        lax.dot_general(
            full_strip,
            rows_here,
            (((0,), (0,)), ((), ())),
            precision=lax.Precision.HIGHEST,
            preferred_element_type=jnp.float32,
        )
        / K,
        "dp",
        scatter_dimension=0,
        tiled=True,
    )
    row_part = lax.dynamic_slice_in_dim(row_scale, lax.axis_index("dp") * strip_rows, strip_rows, 0)
    scaled_rows = rows_here * row_part[:, None] * col_scale[None, :]
    large_sum = jnp.sum(scaled_rows * scaled_rows)
    small_total, large_total = lax.psum((small_sum, large_sum), ("dp", "mp"))
    norm_pair = jnp.stack([small_total, large_total]) / (K * COUT)
    return (output, left_factor, right_factor, norm_pair)


def solution(mesh):
    in_specs = (P("dp", None), P(None, "mp"), P("mp"), P("dp", "mp"), P(), P("mp"))
    out_specs = (P("dp", "mp"), P("dp", "mp"), P("dp", "mp"), P())
    return jax.shard_map(shards, mesh=mesh, in_specs=in_specs, out_specs=out_specs, check_vma=False)
```

profile of v0, /device:TPU:7, one launch (start us, length us, event | category | flops | bytes accessed | tf_op | source)
XLA Modules:
  0.0 346.5 jit_solution(10241874328816004457)
XLA Ops:
  7.2 0.0 copy-start
  7.2 0.0 all-reduce.3.cloned.1.call-start
  7.2 10.4 %multiply_reduce_fusion = (f32[]{:T(128)}, f32[3072,384]{1,0:T(8,128)}) fusion(f32[384]{0:T(512)} %param.11, f32[3072]{0:T(1024)} %param.10, bf16[1152,3072]{1,0:T(8,128)(2,1)} %param.6, bf16[1152,384]{1,0:T(8,128)(2,1)} %param.9), kind=kOutput, calls=%fused_computation | convolution fusion | flops 2722627584 | bytes 12695044 | tf_op jit(solution)/shard_map/dot_general | solution.py:16
  17.6 0.0 all-reduce.3.cloned.1.call-update
  17.7 0.0 all-gather.2.cloned.1.call-start
  17.7 0.8 dynamic_slice.7
  18.5 170.1 %all-reduce.3.cloned.1.call-done = f32[3072,384]{1,0:T(8,128)} async-done(((f32[3072,384]{1,0:T(8,128)}), f32[3072,384]{1,0:T(8,128)}) %all-reduce.3.cloned.1.call-update) | async-done | bytes 4718608 | tf_op jit(solution)/shard_map/psum | solution.py:21
  188.6 0.0 copy-done.2
  188.6 2.6 multiply_reduce_fusion.1
  191.2 0.0 all-gather.2.cloned.1.call-update
  191.2 0.0 reduce-scatter.5.cloned.1.call-start
  191.3 22.7 %all-gather.2.cloned.1.call-done = f32[384,1536]{1,0:T(8,128)} async-done(((f32[384,384]{1,0:T(8,128)}), f32[384,1536]{1,0:T(8,128)}) %all-gather.2.cloned.1.call-update) | async-done | bytes 2359312 | tf_op jit(solution)/shard_map/all_gather | solution.py:31
  214.0 7.2 %convolution_multiply_fusion.1 = f32[1536,384]{1,0:T(8,128)} fusion(f32[384,1536]{1,0:T(8,128)} %all-gather.2.cloned.1.call-done, f32[384,384]{1,0:T(8,128)} %get-tuple-element.7), kind=kOutput, calls=%fused_computation.2 | convolution fusion | flops 2718498816 | bytes 5308416 | tf_op jit(solution)/shard_map/dot_general | solution.py:33
  221.2 0.0 reduce-scatter.5.cloned.1.call-update
  221.3 0.2 reduce-scatter.3.cloned.1.call-start
  221.5 0.0 copy-done.1
  221.5 11.0 %convolution_multiply_fusion = f32[384,3072]{1,0:T(8,128)} fusion(f32[384,384]{1,0:T(8,128)S(1)} %copy-done.1, f32[3072,384]{1,0:T(8,128)} %all-reduce.3.cloned.1.call-done), kind=kOutput, calls=%fused_computation.1 | convolution fusion | flops 5436997632 | bytes 10027008 | tf_op jit(solution)/shard_map/dot_general | solution.py:23
  232.5 0.0 reduce-scatter.3.cloned.1.call-update
  232.5 0.6 copy-done.3
  233.1 7.1 %fusion = bf16[1152,384]{1,0:T(8,128)(2,1)} fusion(bf16[1152,3072]{1,0:T(8,128)(2,1)} %param.6, bf16[3072,384]{1,0:T(8,128)(2,1)S(1)} %copy-done, f32[384]{0:T(512)S(1)} %copy-done.3), kind=kOutput, calls=%fused_computation.4 | convolution fusion | flops 2718793728 | bytes 10323456 | tf_op jit(solution)/shard_map/dot_general | solution.py:11
  240.2 39.4 %all-reduce = (f32[1]{0:T(128)}, f32[1]{0:T(128)}) all-reduce(f32[1]{0:T(128)} %bitcast.1, f32[1]{0:T(128)} %bitcast), channel_id=1, replica_groups=mesh['dp'=8,'mp'=4] {'dp','mp'}, use_global_device_ids=true, to_apply=%region_6.0 | all-reduce | flops 2 | bytes 16 | tf_op jit(solution)/shard_map/psum | solution.py:48
  279.6 1.8 maximum_multiply_fusion
  281.4 8.1 %reduce-scatter.5.cloned.1.call-done = f32[192,384]{1,0:T(8,128)} async-done(((f32[1536,384]{1,0:T(8,128)}), f32[192,384]{1,0:T(8,128)}) %reduce-scatter.5.cloned.1.call-update) | async-done | bytes 294928 | tf_op jit(solution)/shard_map/reduce_scatter | solution.py:32
  289.5 50.5 %reduce-scatter.3.cloned.1.call-done = f32[384,768]{1,0:T(8,128)} async-done(((f32[384,3072]{1,0:T(8,128)}), f32[384,768]{1,0:T(8,128)}) %reduce-scatter.3.cloned.1.call-update) | async-done | bytes 1179664 | tf_op jit(solution)/shard_map/reduce_scatter | solution.py:30
  (4 shorter events, 0.0 us)
Async XLA Ops:
  7.2 225.3 %copy-start = (bf16[3072,384]{1,0:T(8,128)(2,1)S(1)}, bf16[3072,384]{1,0:T(8,128)(2,1)}, u32[]{:S(2)}) copy-start(bf16[3072,384]{1,0:T(8,128)(2,1)} %param.7) | copy-start | bytes 7077892
  7.2 181.4 %all-reduce.3.cloned.1.call-start = ((), (), s32[]{:S(2)}) async-start(), calls=%async_computation.2 | async-start | bytes 9437184 | tf_op jit(solution)/shard_map/psum | solution.py:21
  17.6 171.0 %copy-start.2 = (f32[384]{0:T(512)S(1)}, f32[384]{0:T(512)}, u32[]{:S(2)}) copy-start(f32[384]{0:T(512)} %param.11) | copy-start | bytes 4612
  17.7 196.3 %all-gather.2.cloned.1.call-start = ((), (), s32[]{:S(2)}) async-start(), calls=%async_computation.4 | async-start | bytes 2949120 | tf_op jit(solution)/shard_map/all_gather | solution.py:31
  191.2 30.3 %copy-start.1 = (f32[384,384]{1,0:T(8,128)S(1)}, f32[384,384]{1,0:T(8,128)}, u32[]{:S(2)}) copy-start(f32[384,384]{1,0:T(8,128)} %get-tuple-element.7) | copy-start | bytes 1769476
  191.2 98.3 %reduce-scatter.5.cloned.1.call-start = ((), (), s32[]{:S(2)}) async-start(), calls=%async_computation.5 | async-start | bytes 2654208 | tf_op jit(solution)/shard_map/reduce_scatter | solution.py:32
  221.3 118.7 %reduce-scatter.3.cloned.1.call-start = ((), (), s32[]{:S(2)}) async-start(), calls=%async_computation.3 | async-start | bytes 5898240 | tf_op jit(solution)/shard_map/reduce_scatter | solution.py:30
  232.5 0.7 copy-start.3
Sparse Core Ops, SparseCore 0:
  17.8 170.7 all-reduce.2
  191.3 22.5 all-gather.1
  221.4 68.0 reduce-scatter.4
  292.5 47.4 reduce-scatter.2
where the time goes:
time: 349 us; the launch traced here: 346 us
  waiting for transfers between devices  251 us (72%)
  blocking collectives  39.4 us (11%)
  matrix products  35.7 us (10%)
  between operations  13.8 us (4%)
  other arithmetic  4.38 us (1%)
    psum x1, waiting for transfers between devices, shards(): column = lax.psum(local_grad, 'dp')  170 us
    reduce_scatter x1, waiting for transfers between devices, shards(): lax.psum_scatter(left_part / COUT, 'mp', scatter_dimension=1, tiled=True)  50.5 us
    psum x1, blocking collectives, shards(): small_total, large_total = lax.psum((small_sum, large_sum), ('dp', 'mp'))  39.4 us
    all_gather x1, waiting for transfers between devices, shards(): full_strip = lax.all_gather(rows_here, 'mp', axis=1, tiled=True)  22.7 us
    dot_general x1, matrix products, shards(): lax.dot_general(rows_here, column, (((1,), (1,)), ((), ())), precision=la...  11 us
    dot_general x1, matrix products, shards(): lax.dot_general(patches, cotangent, (((0,), (0,)), ((), ())), preferred_e...  10.4 us
    reduce_scatter x1, waiting for transfers between devices, shards(): lax.psum_scatter(lax.dot_general(full_strip, rows_here, (((0,), (0,)), ((...  8.07 us
    dot_general x1, matrix products, shards(): lax.dot_general(full_strip, rows_here, (((0,), (0,)), ((), ())), precisio...  7.25 us
  transfers between devices with their start and end apart: 4, of which 4 were waited for; matrix products, arithmetic and copies ran while one was open for 6% of the time, Pallas kernels for 0%

commit v1 on v0

--- a/solution.py
+++ b/solution.py
@@ -1,10 +1,18 @@
+import functools
+
 import jax
 import jax.numpy as jnp
 from jax import lax
+from jax.experimental import pallas as pl
+from jax.experimental.pallas import tpu as pltpu
 from jax.sharding import PartitionSpec as P
 
 COUT = 1536
 K = 3072
+F32 = jnp.float32
+BF16 = jnp.bfloat16
+MESH = pl.DeviceIdType.MESH
+FLIPS = ((0, 0), (0, 1), (1, 0), (1, 1))
 
 
 def shards(patches, weight, conv_bias, cotangent, row_scale, col_scale):
@@ -50,7 +58,286 @@
     return (output, left_factor, right_factor, norm_pair)
 
 
+def flip(bit, by):
+    return 1 - bit if by else bit
+
+
+def halves(value):
+    high = value.astype(BF16)
+    return high, (value - high.astype(F32)).astype(BF16)
+
+
+def dot3(a, b, dims):
+    a_high, a_low = a
+    b_high, b_low = b
+    dot = functools.partial(
+        lax.dot_general, dimension_numbers=(dims, ((), ())), preferred_element_type=F32
+    )
+    return dot(a_high, b_high) + (dot(a_high, b_low) + dot(a_low, b_high))
+
+
+def kernel(
+    patches, weight, bias, cot, row_scale, col_scale, output, left, right, norms,
+    grad, got_x, got_z1, got_z2, column, lparts, lcore, ly, bcol, racc, rgot, nown, ngot, fsplit,
+    s_x, r_x, s_z1, r_z1, s_z2, r_z2,
+    s_gx, r_gx, s_gz1, r_gz1, s_gz2, r_gz2,
+    s_lc, r_lc, s_ly, r_ly, s_b1, s_b2, r_b, s_r, r_r, s_n, r_n,
+):
+    d, m = lax.axis_index("dp"), lax.axis_index("mp")
+    x, z0, z1 = d % 2, (d // 2) % 2, d // 4
+    z = d // 2
+    c, y = m % 2, m // 2
+    px = (d + 1 - 2 * x, m)
+    pz1 = (d + 2 - 4 * z0, m)
+    pz2 = (d + 4 - 8 * z1, m)
+    pc = (d, m + 1 - 2 * c)
+    py = (d, m + 2 - 4 * y)
+    size = got_z2.shape[0]
+    half = size // 2
+
+    def zk(k):
+        f1, f0 = FLIPS[k]
+        return 2 * flip(z1, f1) + flip(z0, f0)
+
+    def strip(k, other):
+        at = (zk(k) * 2 + flip(x, other)) * size
+        return pl.ds(pl.multiple_of(at, size), size)
+
+    def copy(src, dst, send, recv, to):
+        return pltpu.make_async_remote_copy(
+            src_ref=src, dst_ref=dst, send_sem=send, recv_sem=recv, device_id=to, device_id_type=MESH
+        )
+
+    barrier = pltpu.get_barrier_semaphore()
+    for to in (px, pz1, pz2, pc, py):
+        pl.semaphore_signal(barrier, inc=1, device_id=to, device_id_type=MESH)
+    nown[...] = jnp.zeros_like(nown)
+    pl.semaphore_wait(barrier, 5)
+
+    def folded(value, rows):
+        scaled = value * row_scale[rows, :] * col_scale[...]
+        return jnp.sum((scaled * scaled).reshape(-1, 8, value.shape[1]), axis=0)
+
+    def make_grad(rows):
+        value = lax.dot_general(
+            patches[:, rows], cot[...], (((0,), (0,)), ((), ())), preferred_element_type=F32
+        )
+        grad[rows, :] = value
+        nown[0, 0:8, :] += folded(value, rows)
+
+    ORDER = (3, 2, 1, 0)
+    xc = [copy(grad.at[strip(k, 1)], got_x.at[k], s_x.at[k], r_x.at[k], px) for k in range(4)]
+    for k in ORDER:
+        make_grad(strip(k, 1))
+        xc[k].start()
+    for k in ORDER:
+        make_grad(strip(k, 0))
+
+    def out_tile(i, _):
+        rows = pl.ds(pl.multiple_of(i * 128, 128), 128)
+        value = jnp.dot(patches[rows, :], weight[...], preferred_element_type=F32) + bias[...]
+        output[rows, :] = value.astype(BF16)
+        return 0
+
+    def out_tiles(a, b):
+        lax.fori_loop(a, b, out_tile, 0)
+
+    tiles = patches.shape[0] // 128
+    out_tiles(0, tiles // 3)
+
+    z1c = [copy(got_x.at[2 * f + 1], got_z1.at[f], s_z1.at[f], r_z1.at[f], pz1) for f in range(2)]
+    z2c = copy(got_z1.at[1], got_z2, s_z2, r_z2, pz2)
+    xc[3].wait_recv()
+    got_x[3] += grad[strip(3, 0), :]
+    z1c[1].start()
+    out_tiles(tiles // 3, 2 * (tiles // 3))
+    xc[2].wait_recv()
+    got_x[2] += grad[strip(2, 0), :]
+    z1c[1].wait_recv()
+    got_z1[1] += got_x[2]
+    z2c.start()
+    out_tiles(2 * (tiles // 3), tiles)
+    xc[1].wait_recv()
+    got_x[1] += grad[strip(1, 0), :]
+    z1c[0].start()
+    xc[0].wait_recv()
+    got_x[0] += grad[strip(0, 0), :]
+    z1c[0].wait_recv()
+    got_x[0] += got_z1[0]
+    z2c.wait_recv()
+    mine = got_x[0] + got_z2[...]
+    own = strip(0, 0)
+    column[own, :] = mine
+    nown[0, 8:16, :] = folded(mine, own)
+    high, low = halves(mine)
+    fsplit[0] = high
+    fsplit[1] = low
+
+    n_to = (px, pz1, pz2, pc, py)
+    nc = [copy(nown.at[i], ngot.at[i], s_n.at[i], r_n.at[i], n_to[i]) for i in range(5)]
+    nc[0].start()
+
+    def col(k, other):
+        return column.at[strip(k, other)]
+
+    gz1 = [copy(col(0, 0), col(0, 0), s_gz1.at[0], r_gz1.at[0], pz1),
+           copy(col(2, 0), col(2, 0), s_gz1.at[1], r_gz1.at[1], pz1)]
+    gz1_in = [copy(col(1, 0), col(1, 0), s_gz1.at[0], r_gz1.at[0], pz1),
+              copy(col(3, 0), col(3, 0), s_gz1.at[1], r_gz1.at[1], pz1)]
+    gz2 = copy(col(0, 0), col(0, 0), s_gz2, r_gz2, pz2)
+    gz2_in = copy(col(2, 0), col(2, 0), s_gz2, r_gz2, pz2)
+    gx = [copy(col(k, 0), col(k, 0), s_gx.at[k], r_gx.at[k], px) for k in range(4)]
+    gx_in = [copy(col(k, 1), col(k, 1), s_gx.at[k], r_gx.at[k], px) for k in range(4)]
+    lcc = [copy(lparts.at[k], lcore.at[k], s_lc.at[k], r_lc.at[k], pc) for k in range(4)]
+    lyc = [copy(lparts.at[k], ly, s_ly, r_ly, py) for k in range(4)]
+    b_core = [copy(col(k, 0), bcol.at[k], s_b1.at[k], r_b.at[k], pc) for k in range(4)]
+    b_y = [copy(col(k, 0), bcol.at[k], s_b2.at[k], r_b.at[k], py) for k in range(4)]
+    b_on = [copy(bcol.at[k], bcol.at[k], s_b1.at[k], r_b.at[k], pc) for k in range(4)]
+    source = m == z
+    relay = py[1] == z
+
+    gz2.start()
+    gz1[0].start()
+    gx[0].start()
+
+    def left_part(k, other):
+        first = (fsplit[0], fsplit[1])
+        value = dot3(first, halves(column[strip(k, other), :]), ((1,), (1,)))
+        at = pl.multiple_of(flip(x, other) * size, size)
+        lparts[k, :, pl.ds(at, size)] = value
+
+    for k in range(4):
+        if k == 1:
+            gz1_in[0].wait_recv()
+            gx[1].start()
+        if k == 2:
+            gz2_in.wait_recv()
+            gz1[1].start()
+            gx[2].start()
+        if k == 3:
+            gz1_in[1].wait_recv()
+            gx[3].start()
+
+        @pl.when(source)
+        def _():
+            b_y[k].start()
+            b_core[k].start()
+            bcol[k] = column[strip(k, 0), :]
+
+        left_part(k, 0)
+
+        @pl.when(jnp.logical_not(source))
+        def _():
+            b_core[k].wait_recv()
+
+        @pl.when(relay)
+        def _():
+            b_on[k].start()
+
+        value = dot3(halves(bcol[k]), halves(column[strip(k, 0), :]), ((0,), (0,)))
+        if k == 0:
+            racc[...] = value
+        else:
+            racc[...] += value
+        if k == 3:
+            r_half = pl.ds(pl.multiple_of((1 - x) * half, half), half)
+            rc = copy(racc.at[r_half], rgot, s_r, r_r, px)
+            rc.start()
+        gx_in[k].wait_recv()
+        left_part(k, 1)
+
+        @pl.when(zk(k) % 2 != c)
+        def _():
+            lcc[k].start()
+
+        @pl.when(zk(k) % 2 == c)
+        def _():
+            lcc[k].wait_recv()
+            lparts[k] += lcore[k]
+
+            @pl.when(zk(k) // 2 != y)
+            def _():
+                lyc[k].start()
+
+        nc[k].wait_recv()
+        nown[k + 1] = nown[k] + ngot[k]
+        nc[k + 1].start()
+
+    rc.wait_recv()
+    right[...] = (racc[pl.ds(pl.multiple_of(x * half, half), half), :] + rgot[...]) * (1.0 / K)
+    nc[4].wait_recv()
+    both = nown[4] + ngot[4]
+    norms[0] = jnp.sum(both[0:8]) / (K * COUT)
+    norms[1] = jnp.sum(both[8:16]) / (K * COUT)
+    lyc[0].wait_recv()
+    kk = 2 * ((z1 + y) % 2) + (z0 + c) % 2
+    left[...] = (lparts[kk] + ly[...]) * (1.0 / COUT)
+
+    for one in (*xc, *z1c, z2c, *gz1, gz2, *gx, rc, *nc):
+        one.wait_send()
+    lyc[0].wait_send()
+    for k in range(4):
+
+        @pl.when(zk(k) % 2 != c)
+        def _():
+            lcc[k].wait_send()
+
+        @pl.when(source)
+        def _():
+            b_y[k].wait_send()
+            b_core[k].wait_send()
+
+        @pl.when(relay)
+        def _():
+            b_on[k].wait_send()
+
+
+def fused(patches, weight, conv_bias, cotangent, row_scale, col_scale):
+    rows, width = patches.shape
+    cols = cotangent.shape[1]
+    size = width // 8
+    vmem = pl.BlockSpec(memory_space=pltpu.VMEM)
+    dma = pltpu.SemaphoreType.DMA
+    one, four = dma, dma((4,))
+    return pl.pallas_call(
+        kernel,
+        out_shape=(
+            jax.ShapeDtypeStruct((rows, cols), BF16),
+            jax.ShapeDtypeStruct((size, width // 4), F32),
+            jax.ShapeDtypeStruct((cols // 2, cols), F32),
+            jax.ShapeDtypeStruct((2,), F32),
+        ),
+        in_specs=[vmem] * 6,
+        out_specs=(vmem, vmem, vmem, pl.BlockSpec(memory_space=pltpu.SMEM)),
+        scratch_shapes=[
+            pltpu.VMEM((width, cols), F32),
+            pltpu.VMEM((4, size, cols), F32),
+            pltpu.VMEM((2, size, cols), F32),
+            pltpu.VMEM((size, cols), F32),
+            pltpu.VMEM((width, cols), F32),
+            pltpu.VMEM((4, size, 2 * size), F32),
+            pltpu.VMEM((4, size, 2 * size), F32),
+            pltpu.VMEM((size, 2 * size), F32),
+            pltpu.VMEM((4, size, cols), F32),
+            pltpu.VMEM((cols, cols), F32),
+            pltpu.VMEM((cols // 2, cols), F32),
+            pltpu.VMEM((5, 16, cols), F32),
+            pltpu.VMEM((5, 16, cols), F32),
+            pltpu.VMEM((2, size, cols), BF16),
+            four, four, dma((2,)), dma((2,)), one, one,
+            four, four, dma((2,)), dma((2,)), one, one,
+            four, four, one, one, four, four, four, one, one, dma((5,)), dma((5,)),
+        ],
+        compiler_params=pltpu.CompilerParams(
+            collective_id=0, has_side_effects=True, vmem_limit_bytes=60 * 1024 * 1024
+        ),
+    )(
+        patches, weight, conv_bias[None, :], cotangent, row_scale[:, None], col_scale[None, :]
+    )
+
+
 def solution(mesh):
     in_specs = (P("dp", None), P(None, "mp"), P("mp"), P("dp", "mp"), P(), P("mp"))
     out_specs = (P("dp", "mp"), P("dp", "mp"), P("dp", "mp"), P())
-    return jax.shard_map(shards, mesh=mesh, in_specs=in_specs, out_specs=out_specs, check_vma=False)
+    body = fused if (mesh.shape["dp"], mesh.shape["mp"]) == (8, 4) else shards
+    return jax.shard_map(body, mesh=mesh, in_specs=in_specs, out_specs=out_specs, check_vma=False)

time: 349 us -> 190 us (0.54)
  the two profiles are of different devices: /device:TPU:7 before, /device:TPU:17 now
where the time goes in v1:
time: 190 us
  Pallas kernels  180 us (95%)
  local copies, waits for them, and re-layouts  9.49 us (5%)
    pallas_call x1, Pallas kernels, fused(): pl.pallas_call(kernel, out_shape=(jax.ShapeDtypeStruct((rows, cols), BF16...  180 us
    unnamed x10, local copies, waits for them, and re-layouts  4.62 us

profile of v1, /device:TPU:17, one launch (start us, length us, event | category | flops | bytes accessed | tf_op | source)
XLA Modules:
  0.0 190.2 jit_solution(3115176532299381517)
XLA Ops:
  0.6 1.2 broadcast_in_dim.9.bias
  1.9 1.2 broadcast_in_dim.11.col_scale
  3.1 2.4 %copy.10.row_scale = f32[3072,1]{1,0:T(8,128)} copy(f32[3072,1]{0,1:T(1,128)} %bitcast.1) | data formatting | bytes 24576 | tf_op jit(solution)/shard_map/broadcast_in_dim | solution.py:335
  5.5 180.1 %shard_map.93 = (bf16[1152,384]{1,0:T(8,128)(2,1)}, f32[384,768]{1,0:T(8,128)}, f32[192,384]{1,0:T(8,128)}, f32[2]{0:T(128)}) custom-call(bf16[1152,3072]{1,0:T(8,128)(2,1)} %patches.1, bf16[3072,384]{1,0:T(8,128)(2,1)} %weight.1, f32[1,384]{1,0:T(1,128)} %broadcast_in_dim.9.bias, bf16[1152,384]{1,0:T(8,128)(2,1)} %cot.1, f32[3072,1]{1,0:T(8,128)} %copy.10.row_scale, ...), custom_call_target="tpu_custom_call" | custom-call | tf_op jit(solution)/shard_map/pallas_call | solution.py:302
  185.6 0.0 copy-start
  185.6 2.3 %copy.15 = bf16[1152,384]{1,0:T(8,128)(2,1)} copy(bf16[1152,384]{1,0:T(8,128)(2,1)} %get-tuple-element.8) | data formatting | bytes 1769472
  187.9 0.0 copy-done
  187.9 0.0 copy-start.1
  187.9 0.0 copy-start.2
  187.9 1.0 copy.16
  188.9 0.1 copy-done.1
  189.0 0.7 copy.17
  189.7 0.0 copy-done.2
  189.7 0.5 copy.18
Async XLA Ops:
  185.6 2.3 %copy-start = (f32[384,768]{1,0:T(8,128)S(1)}, f32[384,768]{1,0:T(8,128)}, u32[]{:S(2)}) copy-start(f32[384,768]{1,0:T(8,128)} %get-tuple-element.9) | copy-start | bytes 3538948
  187.9 1.1 copy-start.1
  187.9 1.8 copy-start.2

commit v2 on v1

v2 whole, which is shorter than its diff:
```python
import functools

import jax
import jax.numpy as jnp
from jax import lax
from jax.experimental import pallas as pl
from jax.experimental.pallas import tpu as pltpu
from jax.sharding import PartitionSpec as P

COUT = 1536
K = 3072
F32 = jnp.float32
BF16 = jnp.bfloat16
MESH = pl.DeviceIdType.MESH


def shards(patches, weight, conv_bias, cotangent, row_scale, col_scale):
    output = (jnp.dot(patches, weight, preferred_element_type=jnp.float32) + conv_bias).astype(
        jnp.bfloat16
    )
    inner_width = patches.shape[1]
    strip_rows = inner_width // lax.axis_size("dp")
    local_grad = lax.dot_general(
        patches, cotangent, (((0,), (0,)), ((), ())), preferred_element_type=jnp.float32
    )
    weighted = local_grad * row_scale[:, None] * col_scale[None, :]
    small_sum = jnp.sum(weighted * weighted)
    column = lax.psum(local_grad, "dp")
    rows_here = lax.dynamic_slice_in_dim(column, lax.axis_index("dp") * strip_rows, strip_rows, 0)
    left_part = lax.dot_general(
        rows_here,
        column,
        (((1,), (1,)), ((), ())),
        precision=lax.Precision.HIGHEST,
        preferred_element_type=jnp.float32,
    )
    left_factor = lax.psum_scatter(left_part / COUT, "mp", scatter_dimension=1, tiled=True)
    full_strip = lax.all_gather(rows_here, "mp", axis=1, tiled=True)
    right_factor = lax.psum_scatter(
        lax.dot_general(
            full_strip,
            rows_here,
            (((0,), (0,)), ((), ())),
            precision=lax.Precision.HIGHEST,
            preferred_element_type=jnp.float32,
        )
        / K,
        "dp",
        scatter_dimension=0,
        tiled=True,
    )
    row_part = lax.dynamic_slice_in_dim(row_scale, lax.axis_index("dp") * strip_rows, strip_rows, 0)
    scaled_rows = rows_here * row_part[:, None] * col_scale[None, :]
    large_sum = jnp.sum(scaled_rows * scaled_rows)
    small_total, large_total = lax.psum((small_sum, large_sum), ("dp", "mp"))
    norm_pair = jnp.stack([small_total, large_total]) / (K * COUT)
    return (output, left_factor, right_factor, norm_pair)


def flip(bit, by):
    return 1 - bit if by else bit


def halves(value):
    high = value.astype(BF16)
    return high, (value - high.astype(F32)).astype(BF16)


def dot3(a, b, dims):
    a_high, a_low = a
    b_high, b_low = b
    dot = functools.partial(
        lax.dot_general, dimension_numbers=(dims, ((), ())), preferred_element_type=F32
    )
    return dot(a_high, b_high) + (dot(a_high, b_low) + dot(a_low, b_high))


def kernel(
    patches, weight, rows2, cot, row_scale, output, left, right, norms,
    grad, got_x, got_p, got_i, column, lparts, lcore, ly, bcol, racc, rgot, nown, ngot, fsplit,
    s_x, r_x, s_p, r_p, s_i, r_i,
    s_gx, r_gx, s_gp, s_gi, r_g,
    s_lc, r_lc, s_ly, r_ly, s_b1, s_b2, r_b, s_r, r_r, s_n, r_n,
):
    d, m = lax.axis_index("dp"), lax.axis_index("mp")
    x, z = d % 2, d // 2
    z0, z1 = z % 2, z // 2
    c, y = m % 2, m // 2
    zs = (z, z + 1 - 2 * z0, 2 - z1, 3 - 3 * z1)
    px = (d + 1 - 2 * x, m)
    pz = (zs[1] * 2 + x, m)
    pi = ((3 - z) * 2 + x, m)
    pc = (d, m + 1 - 2 * c)
    py = (d, m + 2 - 4 * y)
    inner = (z0 + z1) % 2 == 1
    outer = (z0 + z1) % 2 == 0
    size = rgot.shape[1]
    half = rgot.shape[0]

    def strip_at(k, other):
        return zs[k] * 2 + (1 - x if other else x)

    def strip(k, other):
        return pl.ds(pl.multiple_of(strip_at(k, other) * size, size), size)

    def copy(src, dst, send, recv, to):
        return pltpu.make_async_remote_copy(
            src_ref=src, dst_ref=dst, send_sem=send, recv_sem=recv, device_id=to, device_id_type=MESH
        )

    barrier = pltpu.get_barrier_semaphore()
    for to in (px, pz, pi, pc, py):
        pl.semaphore_signal(barrier, inc=1, device_id=to, device_id_type=MESH)
    nown[...] = jnp.zeros_like(nown)
    pl.semaphore_wait(barrier, 5)
    bias = rows2[0:1, :]
    col_square = rows2[1:2, :] * rows2[1:2, :]

    def folded(value, at):
        square = value * value * col_square
        total = jnp.zeros((1, size), F32)
        for b in range(size // 128):
            scale = row_scale[pl.ds(at * (size // 128) + b, 1), :]
            total += dot3(
                halves(scale * scale), halves(square[b * 128:(b + 1) * 128]), ((1,), (0,))
            )
        return total

    def make_grad(k, other):
        rows = strip(k, other)
        grad[rows, :] = lax.dot_general(
            patches[:, rows], cot[...], (((0,), (0,)), ((), ())), preferred_element_type=F32
        )

    ORDER = (3, 2, 1, 0)
    xc = [copy(grad.at[strip(k, 1)], got_x.at[k], s_x.at[k], r_x.at[k], px) for k in range(4)]
    for k in ORDER:
        make_grad(k, 1)
        xc[k].start()
    for k in ORDER:
        make_grad(k, 0)

    def small_norm(s, _):
        rows = pl.ds(pl.multiple_of(s * size, size), size)
        nown[0, 0:1, :] += folded(grad[rows, :], s)
        return 0

    lax.fori_loop(0, 8, small_norm, 0)

    def out_tile(i, _):
        rows = pl.ds(pl.multiple_of(i * 128, 128), 128)
        value = jnp.dot(patches[rows, :], weight[...], preferred_element_type=F32) + bias
        output[rows, :] = value.astype(BF16)
        return 0

    def out_tiles(a, b):
        lax.fori_loop(a, b, out_tile, 0)

    tiles = patches.shape[0] // 128
    cuts = [0, tiles // 3, 2 * (tiles // 3), tiles]

    to_p = {
        k: copy(got_x.at[k], got_p.at[k - 1], s_p.at[k - 1], r_p.at[k - 1], pz) for k in (1, 2, 3)
    }
    to_i = {
        k: copy(got_x.at[k], got_i.at[k - 2], s_i.at[k - 2], r_i.at[k - 2], pi) for k in (2, 3)
    }
    for k in ORDER:
        xc[k].wait_recv()
        got_x[k] += grad[strip(k, 0), :]
        if k >= 1:

            @pl.when(outer)
            def _():
                to_p[k].start()

        if k >= 2:

            @pl.when(inner)
            def _():
                to_p[k].wait_recv()
                got_x[k] += got_p[k - 1]
                to_i[k].start()

            out_tiles(cuts[3 - k], cuts[4 - k])
        if k == 1:

            @pl.when(inner)
            def _():
                to_i[3].wait_recv()
                got_x[1] += got_i[1]
                to_p[1].start()

            out_tiles(cuts[2], cuts[3])
    to_p[1].wait_recv()
    got_x[0] += got_p[0]

    @pl.when(inner)
    def _():
        to_i[2].wait_recv()
        got_x[0] += got_i[0]

    own = strip(0, 0)
    column[own, :] = got_x[0]

    def col(k, other):
        return column.at[strip(k, other)]

    def pass_on(k, recv, send, to):
        return copy(col(k, 0), col(k, 0), send, r_g.at[recv], to)

    gp = [pass_on((0, 2, 3)[j], j + 1, s_gp.at[j], pz) for j in range(3)]
    gi = [pass_on(j, j + 2, s_gi.at[j], pi) for j in range(2)]
    g_in = [pass_on(k, k, s_gp.at[0], pz) for k in range(4)]
    gx = [copy(col(k, 0), col(k, 0), s_gx.at[k], r_gx.at[k], px) for k in range(4)]
    gx_in = [copy(col(k, 1), col(k, 1), s_gx.at[k], r_gx.at[k], px) for k in range(4)]
    units = [(k, o) for k in range(4) for o in range(2)]
    lcc = {
        (k, o): copy(
            lparts.at[k, o], lcore.at[k, o], s_lc.at[2 * k + o], r_lc.at[2 * k + o], pc
        )
        for k, o in units
    }
    lyc = {(k, o): copy(lparts.at[k, o], ly.at[o], s_ly.at[o], r_ly.at[o], py) for k, o in units}
    b_core = [copy(col(k, 0), bcol.at[k], s_b1.at[k], r_b.at[k], pc) for k in range(4)]
    b_y = [copy(col(k, 0), bcol.at[k], s_b2.at[k], r_b.at[k], py) for k in range(4)]
    b_on = [copy(bcol.at[k], bcol.at[k], s_b1.at[k], r_b.at[k], pc) for k in range(4)]
    source = m == z
    relay = py[1] == z

    def arrive(k):
        if k >= 1:
            g_in[k].wait_recv()
        gx[k].start()
        if k == 0:
            gp[0].start()

        @pl.when(inner)
        def _():
            if k <= 1:
                gi[k].start()
            else:
                gp[k - 1].start()

        @pl.when(source)
        def _():
            b_y[k].start()
            b_core[k].start()

    arrive(0)
    high, low = halves(got_x[0])
    fsplit[0] = high
    fsplit[1] = low
    nown[0, 8:9, :] = folded(got_x[0], strip_at(0, 0))
    n_to = (px, pz, pi, pc, py)
    nc = [copy(nown.at[i], ngot.at[i], s_n.at[i], r_n.at[i], n_to[i]) for i in range(5)]
    nc[0].start()
    waiting = []

    def collect():
        if not waiting:
            return
        k, o = waiting.pop(0)

        @pl.when(zs[k] % 2 == c)
        def _():
            lcc[k, o].wait_recv()
            lparts[k, o] += lcore[k, o]

            @pl.when(zs[k] // 2 != y)
            def _():
                lyc[k, o].start()

    def left_unit(k, o):
        if o:
            gx_in[k].wait_recv()
        lparts[k, o] = dot3((fsplit[0], fsplit[1]), halves(column[strip(k, o), :]), ((1,), (1,)))

        @pl.when(zs[k] % 2 != c)
        def _():
            lcc[k, o].start()

        collect()
        waiting.append((k, o))

    def right_unit(k):
        @pl.when(source)
        def _():
            bcol[k] = column[strip(k, 0), :]

        @pl.when(jnp.logical_not(source))
        def _():
            b_core[k].wait_recv()

        @pl.when(relay)
        def _():
            b_on[k].start()

        value = dot3(halves(bcol[k]), halves(column[strip(k, 0), :]), ((0,), (0,)))
        if k == 0:
            racc[...] = value
        else:
            racc[...] += value

    def norm_step(i):
        nc[i].wait_recv()
        nown[i + 1] = nown[i] + ngot[i]
        nc[i + 1].start()

    left_unit(0, 0)
    for k in range(1, 4):
        arrive(k)
        left_unit(k, 0)
        left_unit(k - 1, 1)
        collect()
        right_unit(k - 1)
        norm_step(k - 1)
    left_unit(3, 1)
    collect()
    right_unit(3)
    rc = copy(
        racc.at[pl.ds(pl.multiple_of((1 - x) * half, half), half)], rgot, s_r, r_r, px
    )
    rc.start()
    norm_step(3)
    nc[4].wait_recv()
    both = nown[4] + ngot[4]
    norms[0] = jnp.sum(both[0:8]) / (K * COUT)
    norms[1] = jnp.sum(both[8:16]) / (K * COUT)
    at_k = 0
    for k in range(1, 4):
        at_k = at_k + k * (zs[k] == m).astype(jnp.int32)
    for o in range(2):
        lyc[0, o].wait_recv()
        at = pl.multiple_of((1 - x if o else x) * size, size)
        left[:, pl.ds(at, size)] = (lparts[at_k, o] + ly[o]) * (1.0 / COUT)
    rc.wait_recv()
    right[...] = (racc[pl.ds(pl.multiple_of(x * half, half), half), :] + rgot[...]) * (1.0 / K)

    for one in (*xc, to_p[1], gp[0], *gx, rc, *nc, lyc[0, 0], lyc[0, 1]):
        one.wait_send()

    @pl.when(outer)
    def _():
        to_p[2].wait_send()
        to_p[3].wait_send()

    @pl.when(inner)
    def _():
        for one in (to_i[2], to_i[3], gp[1], gp[2], *gi):
            one.wait_send()

    for k in range(4):

        @pl.when(zs[k] % 2 != c)
        def _():
            lcc[k, 0].wait_send()
            lcc[k, 1].wait_send()

        @pl.when(source)
        def _():
            b_y[k].wait_send()
            b_core[k].wait_send()

        @pl.when(relay)
        def _():
            b_on[k].wait_send()


def fused(patches, weight, conv_bias, cotangent, row_scale, col_scale):
    rows, width = patches.shape
    cols = cotangent.shape[1]
    size = width // 8
    vmem = pl.BlockSpec(memory_space=pltpu.VMEM)
    dma = pltpu.SemaphoreType.DMA
    one, four = dma, dma((4,))
    return pl.pallas_call(
        kernel,
        out_shape=(
            jax.ShapeDtypeStruct((rows, cols), BF16),
            jax.ShapeDtypeStruct((size, width // 4), F32),
            jax.ShapeDtypeStruct((cols // 2, cols), F32),
            jax.ShapeDtypeStruct((2,), F32),
        ),
        in_specs=[vmem] * 5,
        out_specs=(vmem, vmem, vmem, pl.BlockSpec(memory_space=pltpu.SMEM)),
        scratch_shapes=[
            pltpu.VMEM((width, cols), F32),
            pltpu.VMEM((4, size, cols), F32),
            pltpu.VMEM((3, size, cols), F32),
            pltpu.VMEM((2, size, cols), F32),
            pltpu.VMEM((width, cols), F32),
            pltpu.VMEM((4, 2, size, size), F32),
            pltpu.VMEM((4, 2, size, size), F32),
            pltpu.VMEM((2, size, size), F32),
            pltpu.VMEM((4, size, cols), F32),
            pltpu.VMEM((cols, cols), F32),
            pltpu.VMEM((cols // 2, cols), F32),
            pltpu.VMEM((5, 16, cols), F32),
            pltpu.VMEM((5, 16, cols), F32),
            pltpu.VMEM((2, size, cols), BF16),
            four, four, dma((3,)), dma((3,)), dma((2,)), dma((2,)),
            four, four, dma((3,)), dma((2,)), four,
            dma((8,)), dma((8,)), dma((2,)), dma((2,)), four, four, four, one, one,
            dma((5,)), dma((5,)),
        ],
        compiler_params=pltpu.CompilerParams(
            collective_id=0, has_side_effects=True, vmem_limit_bytes=60 * 1024 * 1024
        ),
    )(
        patches, weight, jnp.stack([conv_bias, col_scale]), cotangent, row_scale.reshape(-1, 128)
    )


def solution(mesh):
    in_specs = (P("dp", None), P(None, "mp"), P("mp"), P("dp", "mp"), P(), P("mp"))
    out_specs = (P("dp", "mp"), P("dp", "mp"), P("dp", "mp"), P())
    body = fused if (mesh.shape["dp"], mesh.shape["mp"]) == (8, 4) else shards
    return jax.shard_map(body, mesh=mesh, in_specs=in_specs, out_specs=out_specs, check_vma=False)
```

time: 190 us -> 144 us (0.76)
  the two profiles are of different devices: /device:TPU:17 before, /device:TPU:7 now
where the time goes in v2:
time: 144 us
  Pallas kernels  137 us (95%)
  local copies, waits for them, and re-layouts  5.89 us (4%)
    pallas_call x1, Pallas kernels, fused(): pl.pallas_call(kernel, out_shape=(jax.ShapeDtypeStruct((rows, cols), BF16...  137 us
    unnamed x10, local copies, waits for them, and re-layouts  4.53 us

profile of v2, /device:TPU:7, one launch (start us, length us, event | category | flops | bytes accessed | tf_op | source)
XLA Modules:
  0.0 143.8 jit_solution(16970206464742525415)
XLA Ops:
  0.6 0.7 stack.9
  1.3 0.7 stack.10
  2.0 0.6 pad_maximum_fusion.rows2
  2.6 136.6 %shard_map.93 = (bf16[1152,384]{1,0:T(8,128)(2,1)}, f32[384,768]{1,0:T(8,128)}, f32[192,384]{1,0:T(8,128)}, f32[2]{0:T(128)}) custom-call(bf16[1152,3072]{1,0:T(8,128)(2,1)} %patches.1, bf16[3072,384]{1,0:T(8,128)(2,1)} %weight.1, f32[2,384]{1,0:T(2,128)} %pad_maximum_fusion.rows2, bf16[1152,384]{1,0:T(8,128)(2,1)} %cot.1, f32[24,128]{1,0:T(8,128)} %bitcast.1), custom_call_target="tpu_custom_call" | custom-call | tf_op jit(solution)/shard_map/pallas_call | solution.py:377
  139.2 0.0 copy-start
  139.2 0.0 copy-start.1
  139.2 0.0 copy-start.2
  139.2 2.3 %copy.14 = bf16[1152,384]{1,0:T(8,128)(2,1)} copy(bf16[1152,384]{1,0:T(8,128)(2,1)} %get-tuple-element.8) | data formatting | bytes 1769472
  141.5 0.0 copy-done
  141.5 1.0 copy.15
  142.5 0.0 copy-done.1
  142.5 0.7 copy.16
  143.3 0.0 copy-done.2
  143.3 0.5 copy.17
Async XLA Ops:
  139.2 2.3 %copy-start = (f32[384,768]{1,0:T(8,128)S(1)}, f32[384,768]{1,0:T(8,128)}, u32[]{:S(2)}) copy-start(f32[384,768]{1,0:T(8,128)} %get-tuple-element.9) | copy-start | bytes 3538948
  139.2 3.3 %copy-start.1 = (f32[192,384]{1,0:T(8,128)S(1)}, f32[192,384]{1,0:T(8,128)}, u32[]{:S(2)}) copy-start(f32[192,384]{1,0:T(8,128)} %get-tuple-element.10) | copy-start | bytes 884740
  139.2 4.0 %copy-start.2 = (f32[2]{0:T(128)S(1)}, f32[2]{0:T(128)}, u32[]{:S(2)}) copy-start(f32[2]{0:T(128)} %get-tuple-element.11) | copy-start | bytes 28

commit v3 on v2

--- a/solution.py
+++ b/solution.py
@@ -76,11 +76,12 @@
 
 
 def kernel(
-    patches, weight, rows2, cot, row_scale, output, left, right, norms,
+    patches_in, weight_in, bias_in, cot, row_scale, col_scale, output_out, left, right, norms,
     grad, got_x, got_p, got_i, column, lparts, lcore, ly, bcol, racc, rgot, nown, ngot, fsplit,
     s_x, r_x, s_p, r_p, s_i, r_i,
     s_gx, r_gx, s_gp, s_gi, r_g,
     s_lc, r_lc, s_ly, r_ly, s_b1, s_b2, r_b, s_r, r_r, s_n, r_n,
+    patches, weight, output, load, w_load, o_store,
 ):
     d, m = lax.axis_index("dp"), lax.axis_index("mp")
     x, z = d % 2, d // 2
@@ -111,10 +112,22 @@
     barrier = pltpu.get_barrier_semaphore()
     for to in (px, pz, pi, pc, py):
         pl.semaphore_signal(barrier, inc=1, device_id=to, device_id_type=MESH)
+    ORDER = (3, 2, 1, 0)
+    loads = {}
+    for o in (1, 0):
+        for k in ORDER:
+            rows = strip(k, o)
+            loads[k, o] = pltpu.make_async_copy(
+                patches_in.at[:, rows], patches.at[:, rows], load.at[2 * k + o]
+            )
+            loads[k, o].start()
+    weight_load = pltpu.make_async_copy(weight_in, weight, w_load)
+    weight_load.start()
     nown[...] = jnp.zeros_like(nown)
     pl.semaphore_wait(barrier, 5)
-    bias = rows2[0:1, :]
-    col_square = rows2[1:2, :] * rows2[1:2, :]
+    bias = bias_in[...].reshape(1, size)
+    col_row = col_scale[...].reshape(1, size)
+    col_square = col_row * col_row
 
     def folded(value, at):
         square = value * value * col_square
@@ -128,17 +141,19 @@
 
     def make_grad(k, other):
         rows = strip(k, other)
+        loads[k, other].wait()
         grad[rows, :] = lax.dot_general(
             patches[:, rows], cot[...], (((0,), (0,)), ((), ())), preferred_element_type=F32
         )
 
-    ORDER = (3, 2, 1, 0)
     xc = [copy(grad.at[strip(k, 1)], got_x.at[k], s_x.at[k], r_x.at[k], px) for k in range(4)]
     for k in ORDER:
         make_grad(k, 1)
         xc[k].start()
     for k in ORDER:
         make_grad(k, 0)
+
+    weight_load.wait()
 
     def small_norm(s, _):
         rows = pl.ds(pl.multiple_of(s * size, size), size)
@@ -192,6 +207,8 @@
                 to_p[1].start()
 
             out_tiles(cuts[2], cuts[3])
+            out_copy = pltpu.make_async_copy(output, output_out, o_store)
+            out_copy.start()
     to_p[1].wait_recv()
     got_x[0] += got_p[0]
 
@@ -252,7 +269,7 @@
     fsplit[0] = high
     fsplit[1] = low
     nown[0, 8:9, :] = folded(got_x[0], strip_at(0, 0))
-    n_to = (px, pz, pi, pc, py)
+    n_to = (pc, py, pz, pi, px)
     nc = [copy(nown.at[i], ngot.at[i], s_n.at[i], r_n.at[i], n_to[i]) for i in range(5)]
     nc[0].start()
     waiting = []
@@ -316,13 +333,13 @@
         right_unit(k - 1)
         norm_step(k - 1)
     left_unit(3, 1)
-    collect()
+    norm_step(3)
     right_unit(3)
     rc = copy(
         racc.at[pl.ds(pl.multiple_of((1 - x) * half, half), half)], rgot, s_r, r_r, px
     )
     rc.start()
-    norm_step(3)
+    collect()
     nc[4].wait_recv()
     both = nown[4] + ngot[4]
     norms[0] = jnp.sum(both[0:8]) / (K * COUT)
@@ -337,6 +354,7 @@
     rc.wait_recv()
     right[...] = (racc[pl.ds(pl.multiple_of(x * half, half), half), :] + rgot[...]) * (1.0 / K)
 
+    out_copy.wait()
     for one in (*xc, to_p[1], gp[0], *gx, rc, *nc, lyc[0, 0], lyc[0, 1]):
         one.wait_send()
 
@@ -372,6 +390,7 @@
     cols = cotangent.shape[1]
     size = width // 8
     vmem = pl.BlockSpec(memory_space=pltpu.VMEM)
+    hbm = pl.BlockSpec(memory_space=pl.ANY)
     dma = pltpu.SemaphoreType.DMA
     one, four = dma, dma((4,))
     return pl.pallas_call(
@@ -382,8 +401,8 @@
             jax.ShapeDtypeStruct((cols // 2, cols), F32),
             jax.ShapeDtypeStruct((2,), F32),
         ),
-        in_specs=[vmem] * 5,
-        out_specs=(vmem, vmem, vmem, pl.BlockSpec(memory_space=pltpu.SMEM)),
+        in_specs=[hbm, hbm, vmem, vmem, vmem, vmem],
+        out_specs=(hbm, vmem, vmem, pl.BlockSpec(memory_space=pltpu.SMEM)),
         scratch_shapes=[
             pltpu.VMEM((width, cols), F32),
             pltpu.VMEM((4, size, cols), F32),
@@ -403,12 +422,16 @@
             four, four, dma((3,)), dma((2,)), four,
             dma((8,)), dma((8,)), dma((2,)), dma((2,)), four, four, four, one, one,
             dma((5,)), dma((5,)),
+            pltpu.VMEM((rows, width), BF16),
+            pltpu.VMEM((width, cols), BF16),
+            pltpu.VMEM((rows, cols), BF16),
+            dma((8,)), one, one,
         ],
         compiler_params=pltpu.CompilerParams(
             collective_id=0, has_side_effects=True, vmem_limit_bytes=60 * 1024 * 1024
         ),
     )(
-        patches, weight, jnp.stack([conv_bias, col_scale]), cotangent, row_scale.reshape(-1, 128)
+        patches, weight, conv_bias, cotangent, row_scale.reshape(-1, 128), col_scale
     )
 
 

time: 144 us -> 138 us (0.958)
  Pallas kernels: 137 us -> 133 us
    pallas_call x1, Pallas kernels: 137 us -> 133 us  [fused(): pl.pallas_call(kernel, out_shape=(jax.ShapeDtypeStruct((rows, cols), BF16...]
where the time goes in v3:
time: 138 us
  Pallas kernels  133 us (96%)
  local copies, waits for them, and re-layouts  4.53 us (3%)
    pallas_call x1, Pallas kernels, fused(): pl.pallas_call(kernel, out_shape=(jax.ShapeDtypeStruct((rows, cols), BF16...  133 us
    unnamed x10, local copies, waits for them, and re-layouts  4.53 us

profile of v3, /device:TPU:7, one launch (start us, length us, event | category | flops | bytes accessed | tf_op | source)
XLA Modules:
  0.0 137.8 jit_solution(11731460702200051711)
XLA Ops:
  0.6 132.6 %shard_map.93 = (bf16[1152,384]{1,0:T(8,128)(2,1)}, f32[384,768]{1,0:T(8,128)}, f32[192,384]{1,0:T(8,128)}, f32[2]{0:T(128)}) custom-call(bf16[1152,3072]{1,0:T(8,128)(2,1)} %patches_in.1, bf16[3072,384]{1,0:T(8,128)(2,1)} %weight_in.1, f32[384]{0:T(512)} %bias_in.1, bf16[1152,384]{1,0:T(8,128)(2,1)} %cot.1, f32[24,128]{1,0:T(8,128)} %bitcast.1, f32[384]{0:T(512)} %col_scale.1), custom_call_target="tpu_custom_call" | custom-call | tf_op jit(solution)/shard_map/pallas_call | solution.py:396
  133.2 0.0 copy-start
  133.3 0.0 copy-start.1
  133.3 0.0 copy-start.2
  133.3 2.3 %copy.14 = bf16[1152,384]{1,0:T(8,128)(2,1)} copy(bf16[1152,384]{1,0:T(8,128)(2,1)} %get-tuple-element.8) | data formatting | bytes 1769472
  135.6 0.0 copy-done
  135.6 1.0 copy.15
  136.6 0.0 copy-done.1
  136.6 0.7 copy.16
  137.3 0.0 copy-done.2
  137.3 0.5 copy.17
Async XLA Ops:
  133.2 2.3 %copy-start = (f32[384,768]{1,0:T(8,128)S(1)}, f32[384,768]{1,0:T(8,128)}, u32[]{:S(2)}) copy-start(f32[384,768]{1,0:T(8,128)} %get-tuple-element.9) | copy-start | bytes 3538948
  133.3 3.3 %copy-start.1 = (f32[192,384]{1,0:T(8,128)S(1)}, f32[192,384]{1,0:T(8,128)}, u32[]{:S(2)}) copy-start(f32[192,384]{1,0:T(8,128)} %get-tuple-element.10) | copy-start | bytes 884740
  133.3 4.0 %copy-start.2 = (f32[2]{0:T(128)S(1)}, f32[2]{0:T(128)}, u32[]{:S(2)}) copy-start(f32[2]{0:T(128)} %get-tuple-element.11) | copy-start | bytes 28

commit v4 on v3

--- a/solution.py
+++ b/solution.py
@@ -82,6 +82,7 @@
     s_gx, r_gx, s_gp, s_gi, r_g,
     s_lc, r_lc, s_ly, r_ly, s_b1, s_b2, r_b, s_r, r_r, s_n, r_n,
     patches, weight, output, load, w_load, o_store,
+    bsum, bp, bi, bx, s_bp, r_bp, s_bi, r_bi, s_bx, r_bx,
 ):
     d, m = lax.axis_index("dp"), lax.axis_index("mp")
     x, z = d % 2, d // 2
@@ -103,6 +104,16 @@
 
     def strip(k, other):
         return pl.ds(pl.multiple_of(strip_at(k, other) * size, size), size)
+
+    low = bx.shape[0]
+    top = size - low
+    head = pl.ds(0, top)
+
+    def upper(k, other):
+        return pl.ds(pl.multiple_of(strip_at(k, other) * size, size), top)
+
+    def lower(k, other):
+        return pl.ds(pl.multiple_of(strip_at(k, other) * size + top, low), low)
 
     def copy(src, dst, send, recv, to):
         return pltpu.make_async_remote_copy(
@@ -146,7 +157,7 @@
             patches[:, rows], cot[...], (((0,), (0,)), ((), ())), preferred_element_type=F32
         )
 
-    xc = [copy(grad.at[strip(k, 1)], got_x.at[k], s_x.at[k], r_x.at[k], px) for k in range(4)]
+    xc = [copy(grad.at[upper(k, 1)], got_x.at[k, head], s_x.at[k], r_x.at[k], px) for k in range(4)]
     for k in ORDER:
         make_grad(k, 1)
         xc[k].start()
@@ -155,6 +166,18 @@
 
     weight_load.wait()
 
+    for k in range(4):
+        for o in range(2):
+            bsum[k, o] = grad[lower(k, o), :]
+    b_p = {k: copy(bsum.at[k], bp.at[k - 1], s_bp.at[k - 1], r_bp.at[k - 1], pz) for k in (1, 2, 3)}
+    b_i = {k: copy(bsum.at[k], bi.at[k - 2], s_bi.at[k - 2], r_bi.at[k - 2], pi) for k in (2, 3)}
+    b_x = copy(bsum.at[0, 1], bx, s_bx, r_bx, px)
+
+    @pl.when(outer)
+    def _():
+        for k in ORDER[:3]:
+            b_p[k].start()
+
     def small_norm(s, _):
         rows = pl.ds(pl.multiple_of(s * size, size), size)
         nown[0, 0:1, :] += folded(grad[rows, :], s)
@@ -174,15 +197,35 @@
     tiles = patches.shape[0] // 128
     cuts = [0, tiles // 3, 2 * (tiles // 3), tiles]
 
+    @pl.when(inner)
+    def _():
+        for k in (3, 2):
+            b_p[k].wait_recv()
+            bsum[k] += bp[k - 1]
+            b_i[k].start()
+        b_i[3].wait_recv()
+        bsum[1] += bi[1]
+        b_p[1].start()
+
     to_p = {
-        k: copy(got_x.at[k], got_p.at[k - 1], s_p.at[k - 1], r_p.at[k - 1], pz) for k in (1, 2, 3)
+        k: copy(got_x.at[k, head], got_p.at[k - 1], s_p.at[k - 1], r_p.at[k - 1], pz) for k in (1, 2, 3)
     }
     to_i = {
-        k: copy(got_x.at[k], got_i.at[k - 2], s_i.at[k - 2], r_i.at[k - 2], pi) for k in (2, 3)
+        k: copy(got_x.at[k, head], got_i.at[k - 2], s_i.at[k - 2], r_i.at[k - 2], pi) for k in (2, 3)
     }
     for k in ORDER:
         xc[k].wait_recv()
-        got_x[k] += grad[strip(k, 0), :]
+        got_x[k, head] += grad[upper(k, 0), :]
+        if k == 3:
+            b_p[1].wait_recv()
+            bsum[0] += bp[0]
+
+            @pl.when(inner)
+            def _():
+                b_i[2].wait_recv()
+                bsum[0] += bi[0]
+
+            b_x.start()
         if k >= 1:
 
             @pl.when(outer)
@@ -194,7 +237,7 @@
             @pl.when(inner)
             def _():
                 to_p[k].wait_recv()
-                got_x[k] += got_p[k - 1]
+                got_x[k, head] += got_p[k - 1]
                 to_i[k].start()
 
             out_tiles(cuts[3 - k], cuts[4 - k])
@@ -203,20 +246,22 @@
             @pl.when(inner)
             def _():
                 to_i[3].wait_recv()
-                got_x[1] += got_i[1]
+                got_x[1, head] += got_i[1]
                 to_p[1].start()
 
             out_tiles(cuts[2], cuts[3])
             out_copy = pltpu.make_async_copy(output, output_out, o_store)
             out_copy.start()
     to_p[1].wait_recv()
-    got_x[0] += got_p[0]
+    got_x[0, head] += got_p[0]
 
     @pl.when(inner)
     def _():
         to_i[2].wait_recv()
-        got_x[0] += got_i[0]
-
+        got_x[0, head] += got_i[0]
+
+    b_x.wait_recv()
+    got_x[0, pl.ds(top, low)] = bsum[0, 0] + bx[...]
     own = strip(0, 0)
     column[own, :] = got_x[0]
 
@@ -355,17 +400,19 @@
     right[...] = (racc[pl.ds(pl.multiple_of(x * half, half), half), :] + rgot[...]) * (1.0 / K)
 
     out_copy.wait()
-    for one in (*xc, to_p[1], gp[0], *gx, rc, *nc, lyc[0, 0], lyc[0, 1]):
+    for one in (*xc, b_x, b_p[1], to_p[1], gp[0], *gx, rc, *nc, lyc[0, 0], lyc[0, 1]):
         one.wait_send()
 
     @pl.when(outer)
     def _():
         to_p[2].wait_send()
         to_p[3].wait_send()
+        b_p[2].wait_send()
+        b_p[3].wait_send()
 
     @pl.when(inner)
     def _():
-        for one in (to_i[2], to_i[3], gp[1], gp[2], *gi):
+        for one in (b_i[2], b_i[3], to_i[2], to_i[3], gp[1], gp[2], *gi):
             one.wait_send()
 
     for k in range(4):
@@ -389,6 +436,7 @@
     rows, width = patches.shape
     cols = cotangent.shape[1]
     size = width // 8
+    low = size // 6
     vmem = pl.BlockSpec(memory_space=pltpu.VMEM)
     hbm = pl.BlockSpec(memory_space=pl.ANY)
     dma = pltpu.SemaphoreType.DMA
@@ -406,8 +454,8 @@
         scratch_shapes=[
             pltpu.VMEM((width, cols), F32),
             pltpu.VMEM((4, size, cols), F32),
-            pltpu.VMEM((3, size, cols), F32),
-            pltpu.VMEM((2, size, cols), F32),
+            pltpu.VMEM((3, size - low, cols), F32),
+            pltpu.VMEM((2, size - low, cols), F32),
             pltpu.VMEM((width, cols), F32),
             pltpu.VMEM((4, 2, size, size), F32),
             pltpu.VMEM((4, 2, size, size), F32),
@@ -426,6 +474,11 @@
             pltpu.VMEM((width, cols), BF16),
             pltpu.VMEM((rows, cols), BF16),
             dma((8,)), one, one,
+            pltpu.VMEM((4, 2, low, cols), F32),
+            pltpu.VMEM((3, 2, low, cols), F32),
+            pltpu.VMEM((2, 2, low, cols), F32),
+            pltpu.VMEM((low, cols), F32),
+            dma((3,)), dma((3,)), dma((2,)), dma((2,)), one, one,
         ],
         compiler_params=pltpu.CompilerParams(
             collective_id=0, has_side_effects=True, vmem_limit_bytes=60 * 1024 * 1024

time: 138 us -> 143 us (1.036); the launches traced: 138 us -> 141 us
  Pallas kernels: 133 us -> 136 us
    pallas_call x1, Pallas kernels: 133 us -> 136 us  [fused(): pl.pallas_call(kernel, out_shape=(jax.ShapeDtypeStruct((rows, cols), BF16...]
where the time goes in v4:
time: 143 us; the launch traced here: 141 us
  Pallas kernels  136 us (95%)
  local copies, waits for them, and re-layouts  4.53 us (3%)
    pallas_call x1, Pallas kernels, fused(): pl.pallas_call(kernel, out_shape=(jax.ShapeDtypeStruct((rows, cols), BF16...  136 us
    unnamed x10, local copies, waits for them, and re-layouts  4.53 us

profile of v4, /device:TPU:7, one launch (start us, length us, event | category | flops | bytes accessed | tf_op | source)
XLA Modules:
  0.0 141.1 jit_solution(14130793280382742643)
XLA Ops:
  0.6 135.9 %shard_map.93 = (bf16[1152,384]{1,0:T(8,128)(2,1)}, f32[384,768]{1,0:T(8,128)}, f32[192,384]{1,0:T(8,128)}, f32[2]{0:T(128)}) custom-call(bf16[1152,3072]{1,0:T(8,128)(2,1)} %patches_in.1, bf16[3072,384]{1,0:T(8,128)(2,1)} %weight_in.1, f32[384]{0:T(512)} %bias_in.1, bf16[1152,384]{1,0:T(8,128)(2,1)} %cot.1, f32[24,128]{1,0:T(8,128)} %bitcast.1, f32[384]{0:T(512)} %col_scale.1), custom_call_target="tpu_custom_call" | custom-call | tf_op jit(solution)/shard_map/pallas_call | solution.py:444
  136.6 0.0 copy-start
  136.6 0.0 copy-start.1
  136.6 0.0 copy-start.2
  136.6 2.3 %copy.14 = bf16[1152,384]{1,0:T(8,128)(2,1)} copy(bf16[1152,384]{1,0:T(8,128)(2,1)} %get-tuple-element.8) | data formatting | bytes 1769472
  138.9 0.0 copy-done
  138.9 1.0 copy.15
  139.9 0.0 copy-done.1
  139.9 0.7 copy.16
  140.6 0.0 copy-done.2
  140.6 0.5 copy.17
Async XLA Ops:
  136.6 2.3 %copy-start = (f32[384,768]{1,0:T(8,128)S(1)}, f32[384,768]{1,0:T(8,128)}, u32[]{:S(2)}) copy-start(f32[384,768]{1,0:T(8,128)} %get-tuple-element.9) | copy-start | bytes 3538948
  136.6 3.3 %copy-start.1 = (f32[192,384]{1,0:T(8,128)S(1)}, f32[192,384]{1,0:T(8,128)}, u32[]{:S(2)}) copy-start(f32[192,384]{1,0:T(8,128)} %get-tuple-element.10) | copy-start | bytes 884740
  136.6 4.0 %copy-start.2 = (f32[2]{0:T(128)S(1)}, f32[2]{0:T(128)}, u32[]{:S(2)}) copy-start(f32[2]{0:T(128)} %get-tuple-element.11) | copy-start | bytes 28
